TPU v7x, 512 devices: a whole 4x8x8 slice. The times are simulated.
512 devices in a mesh: row: 16 (over y, core), col: 32 (over x, z).
Axes of the slice: x: 4, y: 8, z: 8, core: 2. Of those that a mesh axis runs over, the one named last changes fastest.
Arguments:
- excitons: float32 [1024, 1024], P('row', 'col'), may hold values from -500 to 500
- valence_energy: float32 [1024], P('row'), may hold values from -3 to -1
- conduction_energy: float32 [1024], P('col'), may hold values from 1 to 3
- psi_valence: float32 [4096, 1024], P('row', 'col'), may hold values from -0.1875 to 0.1875
- psi_conduction: float32 [4096, 1024], P('col', 'row'), may hold values from -0.1875 to 0.1875
- screened: float32 [4096, 4096], P('row', 'col'), may hold values from -0.9 to 0.975, as said below
Outputs:
- next_vector: float32 [1024, 1024], P('row', 'col')
- coefficients: float32 [4], replicated
Inputs may be any that keep to these rules, and one draw needn't show every extreme that they name: symmetric: screened[p, p'] = screened[p', p].
All inputs are finite; a program needn't handle non-finite values.
Results may differ from a plain program's by a relative error of at most 0.0003.
Values sent between devices are 32-bit elements; how exact they have to be, the bound alone decides.
No kernel may reach another device: no remote copies, remote signals or barrier semaphores. Data moves between devices by JAX's collectives and lax.ppermute only.
A program may use at most 64 MiB of HBM per device.

v0:
```python
import functools
import jax
import jax.numpy as jnp
from jax import lax
from jax.sharding import Mesh
from jax.sharding import PartitionSpec as P

NV = 1024
NC = 1024
STEPS = 2
COL = ("col_0", "col_1")
ROW = ("row_0", "row_1")
ROW_COL = ("row_0", "row_1", "col_0", "col_1")
EPS = 1e-06


def copy_for_each(value, axis):
    size = lax.axis_size(axis)
    return lax.all_to_all(
        jnp.broadcast_to(value[None], (size, *value.shape)), axis, 0, 0, tiled=True
    )


def in_order(parts, dim):
    parts = jnp.moveaxis(parts, 0, dim)
    dims = parts.shape
    return parts.reshape(*dims[:dim], dims[dim] * dims[dim + 1], *dims[dim + 2 :])


def gathered_copies(value, axis, dim):
    parts = copy_for_each(value, axis)
    return in_order(parts, dim)


def cut_along(value, dim, size):
    dims = value.shape
    parts = value.reshape(*dims[:dim], size, dims[dim] // size, *dims[dim + 1 :])
    return jnp.moveaxis(parts, dim, 0)


def sum_at_owner(value, axis, dim):
    parts = cut_along(value, dim, lax.axis_size(axis))
    arrived = lax.all_to_all(parts, axis, split_axis=0, concat_axis=0, tiled=True)
    return arrived.sum(axis=0)


def over_axes(value, axes):
    return functools.reduce(lax.psum, axes, value)


def shards(excitons, valence_energy, conduction_energy, psi_valence, psi_conduction, screened):
    high = lax.Precision.HIGHEST
    count = NV * NC
    energy_gap = conduction_energy[None, :] - valence_energy[:, None]
    total = over_axes(jnp.sum(excitons * excitons), ROW_COL)
    vector = excitons / jnp.sqrt(total / count + EPS)
    previous = jnp.zeros_like(vector)
    beta_prev = jnp.zeros((), jnp.float32)
    values = []
    for step in range(STEPS):
        panel_valence = gathered_copies(psi_valence, COL, 1)
        panel_conduction = gathered_copies(psi_conduction, ROW, 1)
        full_rows = gathered_copies(vector, COL, 1)
        image_block = jnp.dot(full_rows, panel_conduction.T, precision=high)
        image_columns = lax.all_gather(image_block, ROW, axis=0, tiled=True)
        points = jnp.dot(panel_valence, image_columns, precision=high)
        weighted = points * screened
        back_valence = sum_at_owner(jnp.dot(panel_valence.T, weighted, precision=high), ROW, 0)
        back_flipped = back_valence.T
        kernel_flipped = sum_at_owner(
            jnp.dot(panel_conduction.T, back_flipped, precision=high), COL, 0
        )
        image = energy_gap * vector - kernel_flipped.T
        cross, square, older = (
            over_axes(jnp.sum(vector * image), ROW_COL),
            over_axes(jnp.sum(image * image), ROW_COL),
            over_axes(jnp.sum(previous * image), ROW_COL),
        )
        alpha = cross / count
        residual = image - alpha * vector - beta_prev * previous
        squared = (
            square / count - alpha * alpha - 2.0 * beta_prev * older / count + beta_prev * beta_prev
        )
        beta = jnp.sqrt(squared + EPS)
        previous = vector
        vector = residual / beta
        beta_prev = beta
        values.append(alpha)
        values.append(beta)
    return (vector, jnp.stack(values))


def solution(mesh):
    finer = Mesh(mesh.devices.reshape(8, 2, 4, 8), ("row_0", "row_1", "col_0", "col_1"))
    placed = (P(ROW, COL), P(ROW), P(COL), P(ROW, COL), P(COL, ROW), P(ROW, COL))
    return jax.shard_map(
        shards, mesh=finer, in_specs=placed, out_specs=(P(ROW, COL), P()), check_vma=False
    )
```

profile of v0, /device:TPU:8, one launch (start us, length us, event | category | flops | bytes accessed | tf_op | source)
XLA Modules:
  0.0 351.9 jit_solution(16004232356385606627)
XLA Ops:
  0.6 1.4 multiply_reduce_fusion.6
  2.0 20.6 %psum.196 = f32[]{:T(128)} all-reduce(f32[]{:T(128)} %multiply_reduce_fusion.6), channel_id=1, replica_groups=mesh['row_0'=8,'row_1'=2,'col_0'=4,'col_1'=8] {'row_0'}, use_global_device_ids=true, to_apply=%region_1.0 | all-reduce | flops 1 | bytes 8 | tf_op jit(solution)/shard_map/psum | solution.py:48
  22.6 3.1 psum.197
  25.7 8.3 %psum.198 = f32[]{:T(128)} all-reduce(f32[]{:T(128)} %psum.197), channel_id=1, replica_groups=mesh['row_0'=8,'row_1'=2,'col_0'=4,'col_1'=8] {'col_0'}, use_global_device_ids=true, to_apply=%region_3.0 | all-reduce | flops 1 | bytes 8 | tf_op jit(solution)/shard_map/psum | solution.py:48
  34.0 22.8 %psum.199 = f32[]{:T(128)} all-reduce(f32[]{:T(128)} %psum.198), channel_id=1, replica_groups=mesh['row_0'=8,'row_1'=2,'col_0'=4,'col_1'=8] {'col_1'}, use_global_device_ids=true, to_apply=%region_4.0 | all-reduce | flops 1 | bytes 8 | tf_op jit(solution)/shard_map/psum | solution.py:48
  57.5 0.1 broadcast_bitcast_fusion.1
  57.6 0.3 reshape.44
  57.9 0.0 copy-start.2
  57.9 14.0 %all_to_all.42 = f32[32,1,2048]{2,1,0:T(1,128)S(1)} all-to-all(f32[32,1,2048]{2,1,0:T(1,128)S(1)} %reshape.44), channel_id=1, replica_groups=mesh['row_0'=8,'row_1'=2,'col_0'=4,'col_1'=8] {'col_0','col_1'}, dimensions={0} | all-to-all | bytes 524288 | tf_op jit(solution)/shard_map/all_to_all | solution.py:19
  72.0 20.4 %all_to_all.43 = f32[16,128,64]{1,2,0:T(8,128)S(1)} all-to-all(f32[16,128,64]{1,2,0:T(8,128)S(1)} %broadcast_in_dim.11), channel_id=1, replica_groups=mesh['row_0'=8,'row_1'=2,'col_0'=4,'col_1'=8] {'row_0','row_1'}, dimensions={0} | all-to-all | bytes 1048576 | tf_op jit(solution)/shard_map/all_to_all | solution.py:19
  92.4 1.1 broadcast_in_dim.12
  93.5 4.7 %all-to-all-start.2 = ((f32[32,256,32]{1,2,0:T(8,128)}), f32[32,256,32]{1,2,0:T(8,128)S(1)}, u32[]{:S(2)}, u32[]{:S(2)}) async-start(f32[32,256,32]{1,2,0:T(8,128)} %broadcast_in_dim.12), calls=%async_computation.2 | async-start | bytes 2097152 | tf_op jit(solution)/shard_map/all_to_all | solution.py:19
  98.1 0.5 broadcast.6
  98.6 1.3 reduce
  99.9 0.2 reshape.45
  100.1 1.0 fusion.4
  101.2 0.0 copy-start.1
  101.2 17.7 %all_gather.6 = f32[1024,128]{1,0:T(8,128)S(1)} all-gather(f32[64,128]{1,0:T(8,128)S(1)} %fusion.4), channel_id=1, replica_groups=mesh['row_0'=8,'row_1'=2,'col_0'=4,'col_1'=8] {'row_0','row_1'}, dimensions={0}, use_global_device_ids=true | all-gather | bytes 557056 | tf_op jit(solution)/shard_map/all_gather | solution.py:65
  118.9 8.2 %all-to-all-done.2 = f32[32,256,32]{1,2,0:T(8,128)S(1)} async-done(((f32[32,256,32]{1,2,0:T(8,128)}), f32[32,256,32]{1,2,0:T(8,128)S(1)}, u32[]{:S(2)}, u32[]{:S(2)}) %all-to-all-start.2) | async-done | bytes 1048608 | tf_op jit(solution)/shard_map/all_to_all | solution.py:19
  127.0 1.8 fusion.1
  128.8 1.2 convolution_bitcast_fusion.1
  130.1 0.2 copy.12
  130.3 20.0 %all_to_all.44 = f32[16,64,128]{2,1,0:T(8,128)S(1)} all-to-all(f32[16,64,128]{2,1,0:T(8,128)S(1)} %bitcast.89), channel_id=1, replica_groups=mesh['row_0'=8,'row_1'=2,'col_0'=4,'col_1'=8] {'row_0','row_1'}, dimensions={0} | all-to-all | bytes 1048576 | tf_op jit(solution)/shard_map/all_to_all | solution.py:43
  150.3 0.7 convolution_bitcast_fusion.3
  151.0 0.2 copy.13
  151.2 0.3 reshape.46
  151.5 17.6 %all_to_all.45 = f32[32,1,2048]{2,1,0:T(1,128)S(1)} all-to-all(f32[32,1,2048]{2,1,0:T(1,128)S(1)} %reshape.46), channel_id=1, replica_groups=mesh['row_0'=8,'row_1'=2,'col_0'=4,'col_1'=8] {'col_0','col_1'}, dimensions={0} | all-to-all | bytes 524288 | tf_op jit(solution)/shard_map/all_to_all | solution.py:43
  169.2 1.3 reduce.1
  170.4 0.2 reshape.47
  170.7 0.1 reduce_sum.101
  170.7 0.6 copy-done.4
  171.3 0.0 copy-done.5
  171.3 0.7 multiply_reduce_fusion.3
  172.1 15.7 %all-reduce.3 = (f32[]{:T(128)}, f32[]{:T(128)}, f32[]{:T(128)}) all-reduce(f32[]{:T(128)} %get-tuple-element.6, f32[]{:T(128)} %get-tuple-element.7, f32[]{:T(128)} %get-tuple-element.5), channel_id=1, replica_groups=mesh['row_0'=8,'row_1'=2,'col_0'=4,'col_1'=8] {'row_0'}, use_global_device_ids=true, to_apply=%region_13.0 | all-reduce | flops 3 | bytes 24 | tf_op jit(solution)/shard_map/psum | solution.py:48
  187.8 3.1 all-reduce.7
  190.9 10.2 %all-reduce.5 = (f32[]{:T(128)}, f32[]{:T(128)}, f32[]{:T(128)}) all-reduce(f32[]{:T(128)} %get-tuple-element.29, f32[]{:T(128)} %get-tuple-element.30, f32[]{:T(128)} %get-tuple-element.31), channel_id=1, replica_groups=mesh['row_0'=8,'row_1'=2,'col_0'=4,'col_1'=8] {'col_0'}, use_global_device_ids=true, to_apply=%region_15.0 | all-reduce | flops 3 | bytes 24 | tf_op jit(solution)/shard_map/psum | solution.py:48
  201.1 17.3 %all-reduce.1 = (f32[]{:T(128)}, f32[]{:T(128)}, f32[]{:T(128)}) all-reduce(f32[]{:T(128)} %get-tuple-element.23, f32[]{:T(128)} %get-tuple-element.24, f32[]{:T(128)} %get-tuple-element.25), channel_id=1, replica_groups=mesh['row_0'=8,'row_1'=2,'col_0'=4,'col_1'=8] {'col_1'}, use_global_device_ids=true, to_apply=%region_16.0 | all-reduce | flops 3 | bytes 24 | tf_op jit(solution)/shard_map/psum | solution.py:48
  221.7 0.1 subtract_divide_fusion.1
  221.8 0.1 broadcast_bitcast_fusion
  221.8 0.3 reshape.48
  222.2 15.4 %all_to_all.46 = f32[32,1,2048]{2,1,0:T(1,128)S(1)} all-to-all(f32[32,1,2048]{2,1,0:T(1,128)S(1)} %reshape.48), channel_id=1, replica_groups=mesh['row_0'=8,'row_1'=2,'col_0'=4,'col_1'=8] {'col_0','col_1'}, dimensions={0} | all-to-all | bytes 524288 | tf_op jit(solution)/shard_map/all_to_all | solution.py:19
  237.5 1.3 reduce.2
  238.8 0.2 reshape.49
  239.0 1.0 fusion.5
  240.0 15.7 %all_gather.7 = f32[1024,128]{1,0:T(8,128)S(1)} all-gather(f32[64,128]{1,0:T(8,128)S(1)} %fusion.5), channel_id=1, replica_groups=mesh['row_0'=8,'row_1'=2,'col_0'=4,'col_1'=8] {'row_0','row_1'}, dimensions={0}, use_global_device_ids=true | all-gather | bytes 557056 | tf_op jit(solution)/shard_map/all_gather | solution.py:65
  255.8 1.8 fusion
  257.6 1.2 convolution_bitcast_fusion
  258.8 0.2 copy.14
  259.0 20.8 %all_to_all.47 = f32[16,64,128]{2,1,0:T(8,128)S(1)} all-to-all(f32[16,64,128]{2,1,0:T(8,128)S(1)} %bitcast.91), channel_id=1, replica_groups=mesh['row_0'=8,'row_1'=2,'col_0'=4,'col_1'=8] {'row_0','row_1'}, dimensions={0} | all-to-all | bytes 1048576 | tf_op jit(solution)/shard_map/all_to_all | solution.py:43
  279.8 0.7 convolution_bitcast_fusion.2
  280.5 0.2 copy.15
  280.7 1.0 reshape.50
  281.7 4.7 %all-to-all-start.7 = ((f32[32,1,2048]{2,1,0:T(1,128)}), f32[32,1,2048]{2,1,0:T(1,128)S(1)}, u32[]{:S(2)}, u32[]{:S(2)}) async-start(f32[32,1,2048]{2,1,0:T(1,128)} %reshape.50), calls=%async_computation.7 | async-start | bytes 524288 | tf_op jit(solution)/shard_map/all_to_all | solution.py:43
  286.4 12.7 %all-to-all-done.7 = f32[32,1,2048]{2,1,0:T(1,128)S(1)} async-done(((f32[32,1,2048]{2,1,0:T(1,128)}), f32[32,1,2048]{2,1,0:T(1,128)S(1)}, u32[]{:S(2)}, u32[]{:S(2)}) %all-to-all-start.7) | async-done | bytes 262176 | tf_op jit(solution)/shard_map/all_to_all | solution.py:43
  299.1 1.3 reduce.3
  300.4 0.2 reshape.51
  300.6 0.1 reduce_sum.106
  300.6 0.7 multiply_reduce_fusion
  301.3 15.7 %all-reduce.2 = (f32[]{:T(128)}, f32[]{:T(128)}, f32[]{:T(128)}) all-reduce(f32[]{:T(128)} %get-tuple-element.3, f32[]{:T(128)} %get-tuple-element.4, f32[]{:T(128)} %get-tuple-element.2), channel_id=1, replica_groups=mesh['row_0'=8,'row_1'=2,'col_0'=4,'col_1'=8] {'row_0'}, use_global_device_ids=true, to_apply=%region_30.0 | all-reduce | flops 3 | bytes 24 | tf_op jit(solution)/shard_map/psum | solution.py:48
  317.0 3.1 all-reduce.6
  320.1 10.2 %all-reduce.4 = (f32[]{:T(128)}, f32[]{:T(128)}, f32[]{:T(128)}) all-reduce(f32[]{:T(128)} %get-tuple-element.26, f32[]{:T(128)} %get-tuple-element.27, f32[]{:T(128)} %get-tuple-element.28), channel_id=1, replica_groups=mesh['row_0'=8,'row_1'=2,'col_0'=4,'col_1'=8] {'col_0'}, use_global_device_ids=true, to_apply=%region_32.0 | all-reduce | flops 3 | bytes 24 | tf_op jit(solution)/shard_map/psum | solution.py:48
  330.3 17.3 %all-reduce = (f32[]{:T(128)}, f32[]{:T(128)}, f32[]{:T(128)}) all-reduce(f32[]{:T(128)} %get-tuple-element.20, f32[]{:T(128)} %get-tuple-element.21, f32[]{:T(128)} %get-tuple-element.22), channel_id=1, replica_groups=mesh['row_0'=8,'row_1'=2,'col_0'=4,'col_1'=8] {'col_1'}, use_global_device_ids=true, to_apply=%region_33.0 | all-reduce | flops 3 | bytes 24 | tf_op jit(solution)/shard_map/psum | solution.py:48
  350.6 0.7 subtract_divide_fusion
  351.3 0.6 pad_maximum_fusion
  (12 shorter events, 0.1 us)
Async XLA Ops:
  0.6 56.9 %copy-start = (f32[64,32]{0,1:T(8,128)S(1)}, f32[64,32]{0,1:T(8,128)}, u32[]{:S(2)}) copy-start(f32[64,32]{0,1:T(8,128)} %param.6) | copy-start | bytes 24580
  57.9 14.0 %copy-start.2 = (f32[128,64]{0,1:T(8,128)S(1)}, f32[128,64]{0,1:T(8,128)}, u32[]{:S(2)}) copy-start(f32[128,64]{0,1:T(8,128)} %param.10) | copy-start | bytes 98308
  72.0 20.4 %copy-start.3 = (f32[256,32]{0,1:T(8,128)S(1)}, f32[256,32]{0,1:T(8,128)}, u32[]{:S(2)}) copy-start(f32[256,32]{0,1:T(8,128)} %param.9) | copy-start | bytes 98308
  93.5 33.5 %all-to-all-start.2 = ((f32[32,256,32]{1,2,0:T(8,128)}), f32[32,256,32]{1,2,0:T(8,128)S(1)}, u32[]{:S(2)}, u32[]{:S(2)}) async-start(f32[32,256,32]{1,2,0:T(8,128)} %broadcast_in_dim.12), calls=%async_computation.2 | async-start | bytes 2097152 | tf_op jit(solution)/shard_map/all_to_all | solution.py:19
  101.2 25.9 %copy-start.1 = (f32[256,128]{1,0:T(8,128)S(1)}, f32[256,128]{1,0:T(8,128)}, u32[]{:S(2)}) copy-start(f32[256,128]{1,0:T(8,128)} %param.11) | copy-start | bytes 393220
  170.6 0.7 copy-start.4
  170.7 0.7 copy-start.5
  281.7 17.4 %all-to-all-start.7 = ((f32[32,1,2048]{2,1,0:T(1,128)}), f32[32,1,2048]{2,1,0:T(1,128)S(1)}, u32[]{:S(2)}, u32[]{:S(2)}) async-start(f32[32,1,2048]{2,1,0:T(1,128)} %reshape.50), calls=%async_computation.7 | async-start | bytes 524288 | tf_op jit(solution)/shard_map/all_to_all | solution.py:43
where the time goes:
time: 353 us; the launch traced here: 352 us
  blocking collectives  289 us (82%)
  waiting for transfers between devices  20.9 us (6%)
  matrix products  9.44 us (3%)
  other arithmetic  9.38 us (3%)
  starting transfers between devices  9.31 us (3%)
  between operations  7.88 us (2%)
  local copies, waits for them, and re-layouts  6.02 us (2%)
    psum x12, blocking collectives, over_axes(): return functools.reduce(lax.psum, axes, value)  147 us
    all_to_all x3, blocking collectives, sum_at_owner(): lax.all_to_all(parts, axis, split_axis=0, concat_axis=0, tiled=True)  58.4 us
    all_to_all x3, blocking collectives, copy_for_each(): lax.all_to_all(jnp.broadcast_to(value[None], (size, *value.shape)), axis,...  49.7 us
    all_gather x2, blocking collectives, shards(): image_columns = lax.all_gather(image_block, ROW, axis=0, tiled=True)  33.4 us
    all_to_all x1, waiting for transfers between devices, sum_at_owner(): lax.all_to_all(parts, axis, split_axis=0, concat_axis=0, tiled=True)  12.7 us
    all_to_all x1, waiting for transfers between devices, copy_for_each(): lax.all_to_all(jnp.broadcast_to(value[None], (size, *value.shape)), axis,...  8.16 us
  transfers between devices with their start and end apart: 2, of which 2 were waited for; matrix products, arithmetic and copies ran while one was open for 1% of the time, Pallas kernels for 0%

commit v1 on v0

--- a/solution.py
+++ b/solution.py
@@ -12,6 +12,13 @@
 ROW = ("row_0", "row_1")
 ROW_COL = ("row_0", "row_1", "col_0", "col_1")
 EPS = 1e-06
+
+
+def gather_over(array, axis, dim):
+    n_dev = lax.axis_size(axis)
+    blocks = jnp.stack([array for _ in range(n_dev)])
+    blocks = lax.all_to_all(blocks, axis, split_axis=0, concat_axis=0)
+    return jnp.concatenate(blocks, axis=dim)
 
 
 def copy_for_each(value, axis):
@@ -62,7 +69,7 @@
         panel_conduction = gathered_copies(psi_conduction, ROW, 1)
         full_rows = gathered_copies(vector, COL, 1)
         image_block = jnp.dot(full_rows, panel_conduction.T, precision=high)
-        image_columns = lax.all_gather(image_block, ROW, axis=0, tiled=True)
+        image_columns = gather_over(image_block, ROW, 0)
         points = jnp.dot(panel_valence, image_columns, precision=high)
         weighted = points * screened
         back_valence = sum_at_owner(jnp.dot(panel_valence.T, weighted, precision=high), ROW, 0)

time: 353 us -> 378 us (1.071)
  blocking collectives: 289 us -> 308 us
  waiting for transfers between devices: 20.9 us -> 25.1 us
    all_to_all x0 -> x2, blocking collectives: none -> 40.4 us  [gather_over(): blocks = lax.all_to_all(blocks, axis, split_axis=0, concat_axis=0)]
    all_gather x2 -> x0, blocking collectives: 33.4 us -> none  [shards(): image_columns = lax.all_gather(image_block, ROW, axis=0, tiled=True)]
    all_to_all x3, blocking collectives: 49.7 us -> 62.8 us  [copy_for_each(): lax.all_to_all(jnp.broadcast_to(value[None], (size, *value.shape)), axis,...]
    all_to_all x1, waiting for transfers between devices: 8.16 us -> 12.4 us  [copy_for_each(): lax.all_to_all(jnp.broadcast_to(value[None], (size, *value.shape)), axis,...]
where the time goes in v1:
time: 378 us; the launch traced here: 377 us
  blocking collectives  308 us (81%)
  waiting for transfers between devices  25.1 us (7%)
  starting transfers between devices  10.9 us (3%)
  matrix products  9.43 us (2%)
  other arithmetic  9.38 us (2%)
  between operations  7.89 us (2%)
  local copies, waits for them, and re-layouts  5.9 us (2%)
    psum x12, blocking collectives, over_axes(): return functools.reduce(lax.psum, axes, value)  147 us
    all_to_all x3, blocking collectives, copy_for_each(): lax.all_to_all(jnp.broadcast_to(value[None], (size, *value.shape)), axis,...  62.8 us
    all_to_all x3, blocking collectives, sum_at_owner(): lax.all_to_all(parts, axis, split_axis=0, concat_axis=0, tiled=True)  57.7 us
    all_to_all x2, blocking collectives, gather_over(): blocks = lax.all_to_all(blocks, axis, split_axis=0, concat_axis=0)  40.4 us
    all_to_all x1, waiting for transfers between devices, sum_at_owner(): lax.all_to_all(parts, axis, split_axis=0, concat_axis=0, tiled=True)  12.7 us
    all_to_all x1, waiting for transfers between devices, copy_for_each(): lax.all_to_all(jnp.broadcast_to(value[None], (size, *value.shape)), axis,...  12.4 us
  transfers between devices with their start and end apart: 2, of which 2 were waited for; matrix products, arithmetic and copies ran while one was open for 1% of the time, Pallas kernels for 0%

profile of v1, /device:TPU:8, one launch (start us, length us, event | category | flops | bytes accessed | tf_op | source)
XLA Modules:
  0.0 376.9 jit_solution(4137694335879759000)
XLA Ops:
  0.6 1.4 multiply_reduce_fusion.6
  2.0 20.6 %psum.196 = f32[]{:T(128)} all-reduce(f32[]{:T(128)} %multiply_reduce_fusion.6), channel_id=1, replica_groups=mesh['row_0'=8,'row_1'=2,'col_0'=4,'col_1'=8] {'row_0'}, use_global_device_ids=true, to_apply=%region_1.0 | all-reduce | flops 1 | bytes 8 | tf_op jit(solution)/shard_map/psum | solution.py:55
  22.6 3.1 psum.197
  25.7 8.3 %psum.198 = f32[]{:T(128)} all-reduce(f32[]{:T(128)} %psum.197), channel_id=1, replica_groups=mesh['row_0'=8,'row_1'=2,'col_0'=4,'col_1'=8] {'col_0'}, use_global_device_ids=true, to_apply=%region_3.0 | all-reduce | flops 1 | bytes 8 | tf_op jit(solution)/shard_map/psum | solution.py:55
  34.0 22.8 %psum.199 = f32[]{:T(128)} all-reduce(f32[]{:T(128)} %psum.198), channel_id=1, replica_groups=mesh['row_0'=8,'row_1'=2,'col_0'=4,'col_1'=8] {'col_1'}, use_global_device_ids=true, to_apply=%region_4.0 | all-reduce | flops 1 | bytes 8 | tf_op jit(solution)/shard_map/psum | solution.py:55
  57.5 0.1 broadcast_bitcast_fusion.1
  57.6 0.3 reshape.56
  57.9 0.0 copy-start.2
  57.9 14.0 %all_to_all.52 = f32[32,1,2048]{2,1,0:T(1,128)S(1)} all-to-all(f32[32,1,2048]{2,1,0:T(1,128)S(1)} %reshape.56), channel_id=1, replica_groups=mesh['row_0'=8,'row_1'=2,'col_0'=4,'col_1'=8] {'col_0','col_1'}, dimensions={0} | all-to-all | bytes 524288 | tf_op jit(solution)/shard_map/all_to_all | solution.py:26
  71.9 0.8 broadcast_in_dim.11
  72.8 6.2 %all-to-all-start.1 = ((f32[16,128,64]{1,2,0:T(8,128)}), f32[16,128,64]{1,2,0:T(8,128)S(1)}, u32[]{:S(2)}, u32[]{:S(2)}) async-start(f32[16,128,64]{1,2,0:T(8,128)} %broadcast_in_dim.11), calls=%async_computation.1 | async-start | bytes 1048576 | tf_op jit(solution)/shard_map/all_to_all | solution.py:26
  79.0 0.5 broadcast.10
  79.5 1.3 reduce
  80.8 0.2 reshape.57
  81.0 12.4 %all-to-all-done.1 = f32[16,128,64]{1,2,0:T(8,128)S(1)} async-done(((f32[16,128,64]{1,2,0:T(8,128)}), f32[16,128,64]{1,2,0:T(8,128)S(1)}, u32[]{:S(2)}, u32[]{:S(2)}) %all-to-all-start.1) | async-done | bytes 524320 | tf_op jit(solution)/shard_map/all_to_all | solution.py:26
  93.3 1.0 fusion.4
  94.4 20.0 %all_to_all.53 = f32[16,64,128]{2,1,0:T(8,128)S(1)} all-to-all(f32[16,64,128]{2,1,0:T(8,128)S(1)} %stack.14), channel_id=1, replica_groups=mesh['row_0'=8,'row_1'=2,'col_0'=4,'col_1'=8] {'row_0','row_1'}, dimensions={0} | all-to-all | bytes 1048576 | tf_op jit(solution)/shard_map/all_to_all | solution.py:20
  114.4 0.1 broadcast_in_dim.12
  114.6 33.5 %all_to_all.54 = f32[32,256,32]{1,2,0:T(8,128)S(1)} all-to-all(f32[32,256,32]{1,2,0:T(8,128)S(1)} %broadcast_in_dim.12), channel_id=1, replica_groups=mesh['row_0'=8,'row_1'=2,'col_0'=4,'col_1'=8] {'col_0','col_1'}, dimensions={0} | all-to-all | bytes 2097152 | tf_op jit(solution)/shard_map/all_to_all | solution.py:26
  148.0 1.8 fusion.1
  149.8 1.2 convolution_bitcast_fusion.1
  151.1 0.2 copy.12
  151.3 20.0 %all_to_all.55 = f32[16,64,128]{2,1,0:T(8,128)S(1)} all-to-all(f32[16,64,128]{2,1,0:T(8,128)S(1)} %bitcast.93), channel_id=1, replica_groups=mesh['row_0'=8,'row_1'=2,'col_0'=4,'col_1'=8] {'row_0','row_1'}, dimensions={0} | all-to-all | bytes 1048576 | tf_op jit(solution)/shard_map/all_to_all | solution.py:50
  171.4 0.7 convolution_bitcast_fusion.3
  172.0 0.2 copy.13
  172.2 0.3 reshape.58
  172.6 17.6 %all_to_all.56 = f32[32,1,2048]{2,1,0:T(1,128)S(1)} all-to-all(f32[32,1,2048]{2,1,0:T(1,128)S(1)} %reshape.58), channel_id=1, replica_groups=mesh['row_0'=8,'row_1'=2,'col_0'=4,'col_1'=8] {'col_0','col_1'}, dimensions={0} | all-to-all | bytes 524288 | tf_op jit(solution)/shard_map/all_to_all | solution.py:50
  190.2 1.3 reduce.1
  191.4 0.2 reshape.59
  191.7 0.1 reduce_sum.101
  191.8 0.6 copy-done.4
  192.3 0.0 copy-done.5
  192.3 0.7 multiply_reduce_fusion.3
  193.1 15.7 %all-reduce.3 = (f32[]{:T(128)}, f32[]{:T(128)}, f32[]{:T(128)}) all-reduce(f32[]{:T(128)} %get-tuple-element.6, f32[]{:T(128)} %get-tuple-element.7, f32[]{:T(128)} %get-tuple-element.5), channel_id=1, replica_groups=mesh['row_0'=8,'row_1'=2,'col_0'=4,'col_1'=8] {'row_0'}, use_global_device_ids=true, to_apply=%region_13.0 | all-reduce | flops 3 | bytes 24 | tf_op jit(solution)/shard_map/psum | solution.py:55
  208.8 3.1 all-reduce.7
  211.9 10.2 %all-reduce.5 = (f32[]{:T(128)}, f32[]{:T(128)}, f32[]{:T(128)}) all-reduce(f32[]{:T(128)} %get-tuple-element.29, f32[]{:T(128)} %get-tuple-element.30, f32[]{:T(128)} %get-tuple-element.31), channel_id=1, replica_groups=mesh['row_0'=8,'row_1'=2,'col_0'=4,'col_1'=8] {'col_0'}, use_global_device_ids=true, to_apply=%region_15.0 | all-reduce | flops 3 | bytes 24 | tf_op jit(solution)/shard_map/psum | solution.py:55
  222.2 17.3 %all-reduce.1 = (f32[]{:T(128)}, f32[]{:T(128)}, f32[]{:T(128)}) all-reduce(f32[]{:T(128)} %get-tuple-element.23, f32[]{:T(128)} %get-tuple-element.24, f32[]{:T(128)} %get-tuple-element.25), channel_id=1, replica_groups=mesh['row_0'=8,'row_1'=2,'col_0'=4,'col_1'=8] {'col_1'}, use_global_device_ids=true, to_apply=%region_16.0 | all-reduce | flops 3 | bytes 24 | tf_op jit(solution)/shard_map/psum | solution.py:55
  242.7 0.1 subtract_divide_fusion.1
  242.8 0.1 broadcast_bitcast_fusion
  242.8 0.3 reshape.60
  243.2 15.4 %all_to_all.57 = f32[32,1,2048]{2,1,0:T(1,128)S(1)} all-to-all(f32[32,1,2048]{2,1,0:T(1,128)S(1)} %reshape.60), channel_id=1, replica_groups=mesh['row_0'=8,'row_1'=2,'col_0'=4,'col_1'=8] {'col_0','col_1'}, dimensions={0} | all-to-all | bytes 524288 | tf_op jit(solution)/shard_map/all_to_all | solution.py:26
  258.5 1.3 reduce.2
  259.8 0.2 reshape.61
  260.0 1.0 fusion.5
  261.1 20.4 %all_to_all.58 = f32[16,64,128]{2,1,0:T(8,128)S(1)} all-to-all(f32[16,64,128]{2,1,0:T(8,128)S(1)} %stack.15), channel_id=1, replica_groups=mesh['row_0'=8,'row_1'=2,'col_0'=4,'col_1'=8] {'row_0','row_1'}, dimensions={0} | all-to-all | bytes 1048576 | tf_op jit(solution)/shard_map/all_to_all | solution.py:20
  281.5 1.8 fusion
  283.3 1.2 convolution_bitcast_fusion
  284.6 0.2 copy.14
  284.8 20.0 %all_to_all.59 = f32[16,64,128]{2,1,0:T(8,128)S(1)} all-to-all(f32[16,64,128]{2,1,0:T(8,128)S(1)} %bitcast.95), channel_id=1, replica_groups=mesh['row_0'=8,'row_1'=2,'col_0'=4,'col_1'=8] {'row_0','row_1'}, dimensions={0} | all-to-all | bytes 1048576 | tf_op jit(solution)/shard_map/all_to_all | solution.py:50
  304.8 0.7 convolution_bitcast_fusion.2
  305.5 0.2 copy.15
  305.7 1.0 reshape.62
  306.7 4.7 %all-to-all-start.9 = ((f32[32,1,2048]{2,1,0:T(1,128)}), f32[32,1,2048]{2,1,0:T(1,128)S(1)}, u32[]{:S(2)}, u32[]{:S(2)}) async-start(f32[32,1,2048]{2,1,0:T(1,128)} %reshape.62), calls=%async_computation.9 | async-start | bytes 524288 | tf_op jit(solution)/shard_map/all_to_all | solution.py:50
  311.4 12.7 %all-to-all-done.9 = f32[32,1,2048]{2,1,0:T(1,128)S(1)} async-done(((f32[32,1,2048]{2,1,0:T(1,128)}), f32[32,1,2048]{2,1,0:T(1,128)S(1)}, u32[]{:S(2)}, u32[]{:S(2)}) %all-to-all-start.9) | async-done | bytes 262176 | tf_op jit(solution)/shard_map/all_to_all | solution.py:50
  324.1 1.3 reduce.3
  325.3 0.2 reshape.63
  325.6 0.1 reduce_sum.106
  325.6 0.7 multiply_reduce_fusion
  326.3 15.7 %all-reduce.2 = (f32[]{:T(128)}, f32[]{:T(128)}, f32[]{:T(128)}) all-reduce(f32[]{:T(128)} %get-tuple-element.3, f32[]{:T(128)} %get-tuple-element.4, f32[]{:T(128)} %get-tuple-element.2), channel_id=1, replica_groups=mesh['row_0'=8,'row_1'=2,'col_0'=4,'col_1'=8] {'row_0'}, use_global_device_ids=true, to_apply=%region_30.0 | all-reduce | flops 3 | bytes 24 | tf_op jit(solution)/shard_map/psum | solution.py:55
  342.0 3.1 all-reduce.6
  345.1 10.2 %all-reduce.4 = (f32[]{:T(128)}, f32[]{:T(128)}, f32[]{:T(128)}) all-reduce(f32[]{:T(128)} %get-tuple-element.26, f32[]{:T(128)} %get-tuple-element.27, f32[]{:T(128)} %get-tuple-element.28), channel_id=1, replica_groups=mesh['row_0'=8,'row_1'=2,'col_0'=4,'col_1'=8] {'col_0'}, use_global_device_ids=true, to_apply=%region_32.0 | all-reduce | flops 3 | bytes 24 | tf_op jit(solution)/shard_map/psum | solution.py:55
  355.3 17.3 %all-reduce = (f32[]{:T(128)}, f32[]{:T(128)}, f32[]{:T(128)}) all-reduce(f32[]{:T(128)} %get-tuple-element.20, f32[]{:T(128)} %get-tuple-element.21, f32[]{:T(128)} %get-tuple-element.22), channel_id=1, replica_groups=mesh['row_0'=8,'row_1'=2,'col_0'=4,'col_1'=8] {'col_1'}, use_global_device_ids=true, to_apply=%region_33.0 | all-reduce | flops 3 | bytes 24 | tf_op jit(solution)/shard_map/psum | solution.py:55
  375.6 0.7 subtract_divide_fusion
  376.3 0.6 pad_maximum_fusion
  (14 shorter events, 0.2 us)
Async XLA Ops:
  0.6 56.9 %copy-start = (f32[64,32]{0,1:T(8,128)S(1)}, f32[64,32]{0,1:T(8,128)}, u32[]{:S(2)}) copy-start(f32[64,32]{0,1:T(8,128)} %param.6) | copy-start | bytes 24580
  57.9 14.0 %copy-start.2 = (f32[128,64]{0,1:T(8,128)S(1)}, f32[128,64]{0,1:T(8,128)}, u32[]{:S(2)}) copy-start(f32[128,64]{0,1:T(8,128)} %param.10) | copy-start | bytes 98308
  72.8 20.6 %all-to-all-start.1 = ((f32[16,128,64]{1,2,0:T(8,128)}), f32[16,128,64]{1,2,0:T(8,128)S(1)}, u32[]{:S(2)}, u32[]{:S(2)}) async-start(f32[16,128,64]{1,2,0:T(8,128)} %broadcast_in_dim.11), calls=%async_computation.1 | async-start | bytes 1048576 | tf_op jit(solution)/shard_map/all_to_all | solution.py:26
  94.4 20.0 %copy-start.3 = (f32[256,32]{0,1:T(8,128)S(1)}, f32[256,32]{0,1:T(8,128)}, u32[]{:S(2)}) copy-start(f32[256,32]{0,1:T(8,128)} %param.9) | copy-start | bytes 98308
  114.6 33.5 %copy-start.1 = (f32[256,128]{1,0:T(8,128)S(1)}, f32[256,128]{1,0:T(8,128)}, u32[]{:S(2)}) copy-start(f32[256,128]{1,0:T(8,128)} %param.11) | copy-start | bytes 393220
  191.7 0.7 copy-start.4
  191.7 0.7 copy-start.5
  306.7 17.4 %all-to-all-start.9 = ((f32[32,1,2048]{2,1,0:T(1,128)}), f32[32,1,2048]{2,1,0:T(1,128)S(1)}, u32[]{:S(2)}, u32[]{:S(2)}) async-start(f32[32,1,2048]{2,1,0:T(1,128)} %reshape.62), calls=%async_computation.9 | async-start | bytes 524288 | tf_op jit(solution)/shard_map/all_to_all | solution.py:50
